TPU v7x, 256 devices: a whole 4x4x8 slice. The times are simulated.
256 devices in a mesh: tm: 32 (over z, x), rows: 8 (over y, core).
Axes of the slice: x: 4, y: 4, z: 8, core: 2. Of those that a mesh axis runs over, the one named last changes fastest.
Arguments:
- x_start: float32 [1, 16, 128, 128], P(None, None, 'rows'), may hold values from -6 to 6
- noise: float32 [32, 1, 16, 128, 128], P('tm', None, None, 'rows'), may hold values from -6 to 6
- fresh: float32 [5, 1, 16, 128, 128], P(None, None, None, 'rows'), may hold values from -6 to 6
- sched: int32 [38], replicated, may hold values from 888 to 999, as said below
- conv_in: bfloat16 [3, 3, 192, 16], replicated, may hold values from -0.5 to 0.5
- conv_mid: bfloat16 [3, 3, 192, 192], replicated, may hold values from -0.15625 to 0.15625
- conv_out: bfloat16 [3, 3, 16, 192], replicated, may hold values from -0.15625 to 0.15625
- time_weight: bfloat16 [192, 192], replicated, may hold values from -0.4375 to 0.4375
Outputs:
- trajectory: float32 [2, 32, 1, 16, 128, 128], P(None, 'tm', None, None, 'rows')
Inputs may be any that keep to these rules, and one draw needn't show every extreme that they name: sched[0] = 999 and each entry is 1 to 3 below the one before it.
All inputs are finite; a program needn't handle non-finite values.
Results may differ from a plain program's by a relative error of at most 0.00055.
Values may be sent and summed in bfloat16 or wider, within the bound.
No kernel may reach another device: no remote copies, remote signals or barrier semaphores. Data moves between devices by JAX's collectives and lax.ppermute only.
A program may use at most 64 MiB of HBM per device.

v0:
```python
import jax
import jax.numpy as jnp
from jax import lax
from jax.sharding import PartitionSpec as P

STEPS = 1000
SWEEPS = 2
RETIRE = 5
ROUNDS = 2
log_base = 9.210340371976184


def extended(array, sides, width):
    for axis, dim in sides:
        size, length = (lax.axis_size(axis), array.shape[dim])
        up = [(i, (i + 1) % size) for i in range(size - 1)]
        down = [(j, i) for i, j in up]
        last = lax.slice_in_dim(array, length - width, length, axis=dim)
        initial = lax.slice_in_dim(array, 0, width, axis=dim)
        before = lax.ppermute(last, axis, up)
        after = lax.ppermute(initial, axis, down)
        array = jnp.concatenate([before, array, after], axis=dim)
    return array


def entering_2(value, axis, join, neutral):
    count, mine = (lax.axis_size(axis), lax.axis_index(axis))
    pieces = lax.all_gather(value, axis)
    subtotal = jnp.full_like(value, 0) + jnp.asarray(neutral, value.dtype)

    def turn(position, subtotal):
        longer = join(subtotal, pieces[position])
        return jnp.where(position < mine, longer, subtotal)

    return lax.fori_loop(0, count - 1, turn, subtotal)


def from_behind(array, axis, by):
    length = lax.axis_size(axis)
    pairs = [(i, i + by) for i in range(length) if 0 <= i + by < length]
    return lax.ppermute(array, axis, pairs)


def broadcast(value, axis, source):
    kept = jnp.where(lax.axis_index(axis) == source, value, 0).astype(value.dtype)
    return lax.psum(kept, axis)


def plan_table(total_steps):
    positions = jnp.arange(total_steps).astype(jnp.float32)
    betas = 0.0001 + (0.02 - 0.0001) * positions / (total_steps - 1)
    return jnp.cumsum(jnp.log(1.0 - betas))


def lookup(table, position):
    return jnp.sum(jnp.where(jnp.arange(table.shape[0]) == position, table, 0.0))


def coefficients(log_now, log_next):
    retained = jnp.exp(log_now - log_next)
    bar_now = jnp.exp(log_now)
    bar_next = jnp.exp(log_next)
    keep = 1.0 / jnp.sqrt(retained) - 1.0
    predict = -(1.0 - retained) / (jnp.sqrt(1.0 - bar_now) * jnp.sqrt(retained))
    spread = jnp.sqrt((1.0 - bar_next) / (1.0 - bar_now) * (1.0 - retained))
    return (keep, predict, spread)


def time_features(now_value, width):
    half = width // 2
    freqs = jnp.exp(-log_base * jnp.arange(half).astype(jnp.float32) / half)
    angles = now_value * freqs
    return jnp.concatenate([jnp.sin(angles), jnp.cos(angles)], axis=-1)


def convolve(padded, weight, out_rows):
    columns = padded.shape[3]
    widened = jnp.pad(padded, ((0, 0), (0, 0), (0, 0), (1, 1)))
    running = None
    for row_tap in range(3):
        for col_tap in range(3):
            shifted = widened[:, :, row_tap : row_tap + out_rows, col_tap : col_tap + columns]
            product_term = jnp.einsum(
                "oc,fcrw->forw",
                weight[row_tap, col_tap],
                shifted,
                preferred_element_type=jnp.float32,
            )
            running = product_term if running is None else running + product_term
    return running


def hidden_rim(values):
    return extended(values, (("rows", 2),), 1)


def drift_network(state, noise_now, keep, predict, spread, embedding, conv_in, conv_mid, conv_out):
    latent = state[0].astype(jnp.bfloat16)
    strip_rows = latent.shape[2]
    padded = extended(latent, (("rows", 2),), 1)
    first = convolve(padded, conv_in, strip_rows) + embedding[None, :, None, None]
    first = jax.nn.silu(first).astype(jnp.bfloat16)
    second = jax.nn.silu(convolve(hidden_rim(first), conv_mid, strip_rows)).astype(jnp.bfloat16)
    predicted = convolve(hidden_rim(second), conv_out, strip_rows)
    return keep * state + predict * predicted[None] + spread * noise_now


def add_terms(earlier, later):
    return earlier + later


def prefix(change):
    return entering_2(change, "tm", add_terms, jnp.zeros_like(change))


def shards(x_start, noise, fresh, sched, conv_in, conv_mid, conv_out, time_weight):
    slot = lax.axis_index("tm")
    slots = lax.axis_size("tm")
    table = plan_table(STEPS)
    hidden_width = conv_mid.shape[2]
    state = x_start[None]
    noise_now = noise
    base_state = state
    snapshots = []
    for round_index in range(ROUNDS):
        position = slot + RETIRE * round_index
        now_step = lax.dynamic_index_in_dim(sched, position, 0, keepdims=False)
        next_step = lax.dynamic_index_in_dim(sched, position + 1, 0, keepdims=False)
        keep, predict, spread = coefficients(lookup(table, now_step), lookup(table, next_step))
        features = time_features(now_step.astype(jnp.float32), hidden_width)
        embedding = jnp.dot(
            features[None], time_weight.astype(jnp.float32), precision=lax.Precision.HIGHEST
        )[0]
        for sweep_index in range(SWEEPS):
            change = drift_network(
                state, noise_now, keep, predict, spread, embedding, conv_in, conv_mid, conv_out
            )
            state = base_state + prefix(change)
        snapshots.append(state)
        if round_index + 1 < ROUNDS:
            moved_state, moved_noise = from_behind((state, noise_now), "tm", -RETIRE)
            entering = slot >= slots - RETIRE
            pick = jnp.clip(round_index * RETIRE + slot - (slots - RETIRE), 0, fresh.shape[0] - 1)
            incoming = lax.dynamic_index_in_dim(fresh, pick, 0, keepdims=True)
            state = jnp.where(entering, state, moved_state)
            noise_now = jnp.where(entering, incoming, moved_noise)
            base_state = broadcast(state, "tm", 0)
    return jnp.stack(snapshots)


def solution(mesh):
    placed = (
        P(None, None, "rows", None),
        P("tm", None, None, "rows", None),
        P(None, None, None, "rows", None),
        P(),
        P(),
        P(),
        P(),
        P(),
    )
    return jax.shard_map(
        shards,
        mesh=mesh,
        in_specs=placed,
        out_specs=P(None, "tm", None, None, "rows", None),
        check_vma=False,
    )
```

profile of v0, /device:TPU:8, one launch (start us, length us, event | category | flops | bytes accessed | tf_op | source)
XLA Modules:
  0.0 735.1 jit_solution(4137733619743370829)
XLA Ops:
  9.5 3.6 collective-permute-start.1
  17.2 3.2 select_reduce_fusion
  29.3 3.6 collective-permute-start.3
  39.6 3.6 collective-permute-start.4
  43.3 2.5 collective-permute-start.5
  51.6 85.8 %all-gather.9.cloned.1.call-done = f32[32,1,16,16,128]{4,3,2,1,0:T(8,128)} async-done(((f32[1,1,16,16,128]{4,3,2,1,0:T(8,128)}), f32[32,1,16,16,128]{4,3,2,1,0:T(8,128)}) %all-gather.9.cloned.1.call-update) | async-done | bytes 4194320 | tf_op jit(solution)/shard_map/all_gather | solution.py:28
  137.3 30.1 %while.56 = (s32[]{:T(128)}, f32[1,1,16,16,128]{4,3,2,1,0:T(8,128)S(1)}, s32[]{:T(128)}, f32[32,1,1,16,16,128]{5,4,3,2,1,0:T(8,128)}, s32[]{:T(128)}, /*index=5*/s32[]{:T(128)}) while((s32[]{:T(128)}, f32[1,1,16,16,128]{4,3,2,1,0:T(8,128)S(1)}, s32[]{:T(128)}, f32[32,1,1,16,16,128]{5,4,3,2,1,0:T(8,128)}, s32[]{:T(128)}, ...), condition=%wide.region_5.6_spmd.clone, body=%wide.region_4.5_spmd.clone.sunk | while | flops 98308 | bytes 393309 | solution.py:35
  169.5 3.6 collective-permute-start.7
  178.6 3.5 collective-permute-start.8
  190.9 3.5 collective-permute-start.10
  204.3 77.6 %all-gather.11.cloned.1.call-done = f32[32,1,16,16,128]{4,3,2,1,0:T(8,128)} async-done(((f32[1,1,16,16,128]{4,3,2,1,0:T(8,128)}), f32[32,1,16,16,128]{4,3,2,1,0:T(8,128)}) %all-gather.11.cloned.1.call-update) | async-done | bytes 4194320 | tf_op jit(solution)/shard_map/all_gather | solution.py:28
  281.9 30.1 %while.57 = (s32[]{:T(128)}, f32[1,1,16,16,128]{4,3,2,1,0:T(8,128)S(1)}, s32[]{:T(128)}, f32[32,1,1,16,16,128]{5,4,3,2,1,0:T(8,128)}, s32[]{:T(128)}, /*index=5*/s32[]{:T(128)}) while((s32[]{:T(128)}, f32[1,1,16,16,128]{4,3,2,1,0:T(8,128)S(1)}, s32[]{:T(128)}, f32[32,1,1,16,16,128]{5,4,3,2,1,0:T(8,128)}, s32[]{:T(128)}, ...), condition=%wide.region_7.8_spmd.clone, body=%wide.region_6.7_spmd.clone.sunk | while | flops 98308 | bytes 393309 | solution.py:35
  316.5 3.4 collective-permute-done.12
  321.9 3.6 collective-permute-start.14
  331.0 3.5 collective-permute-start.15
  343.2 3.5 collective-permute-start.17
  355.4 82.0 %all-gather.13.cloned.1.call-done = f32[32,1,16,16,128]{4,3,2,1,0:T(8,128)} async-done(((f32[1,1,16,16,128]{4,3,2,1,0:T(8,128)}), f32[32,1,16,16,128]{4,3,2,1,0:T(8,128)}) %all-gather.13.cloned.1.call-update) | async-done | bytes 4194320 | tf_op jit(solution)/shard_map/all_gather | solution.py:28
  437.3 30.1 %while.58 = (s32[]{:T(128)}, f32[1,1,16,16,128]{4,3,2,1,0:T(8,128)S(1)}, s32[]{:T(128)}, f32[32,1,1,16,16,128]{5,4,3,2,1,0:T(8,128)}, s32[]{:T(128)}, /*index=5*/s32[]{:T(128)}) while((s32[]{:T(128)}, f32[1,1,16,16,128]{4,3,2,1,0:T(8,128)S(1)}, s32[]{:T(128)}, f32[32,1,1,16,16,128]{5,4,3,2,1,0:T(8,128)}, s32[]{:T(128)}, ...), condition=%wide.region_12.13_spmd.clone, body=%wide.region_11.12_spmd.clone.sunk | while | flops 98308 | bytes 393309 | solution.py:35
  467.5 112.5 %all-reduce.15.cloned.1.call-done = f32[1,1,16,16,128]{4,2,3,1,0:T(8,128)} async-done(((f32[1,1,16,16,128]{4,2,3,1,0:T(8,128)}), f32[1,1,16,16,128]{4,2,3,1,0:T(8,128)}) %all-reduce.15.cloned.1.call-update) | async-done | bytes 131088 | tf_op jit(solution)/shard_map/psum | solution.py:46
  582.9 3.6 collective-permute-start.21
  592.0 3.5 collective-permute-start.22
  604.2 3.5 collective-permute-start.24
  616.0 81.2 %all-gather.15.cloned.1.call-done = f32[32,1,16,16,128]{4,3,2,1,0:T(8,128)} async-done(((f32[1,1,16,16,128]{4,3,2,1,0:T(8,128)}), f32[32,1,16,16,128]{4,3,2,1,0:T(8,128)}) %all-gather.15.cloned.1.call-update) | async-done | bytes 4194320 | tf_op jit(solution)/shard_map/all_gather | solution.py:28
  697.2 30.2 %while.59 = (s32[]{:T(128)}, f32[1,1,16,16,128]{4,3,2,1,0:T(8,128)S(1)}, s32[]{:T(128)}, f32[32,1,1,16,16,128]{5,4,3,2,1,0:T(8,128)}, s32[]{:T(128)}, /*index=5*/s32[]{:T(128)}) while((s32[]{:T(128)}, f32[1,1,16,16,128]{4,3,2,1,0:T(8,128)S(1)}, s32[]{:T(128)}, f32[32,1,1,16,16,128]{5,4,3,2,1,0:T(8,128)}, s32[]{:T(128)}, ...), condition=%wide.region_14.15_spmd.clone, body=%wide.region_13.14_spmd.clone.sunk | while | flops 98308 | bytes 393309 | solution.py:35
  (355 shorter events, 220.2 us)
Async XLA Ops:
  6.5 130.8 %all-gather.9.cloned.1.call-start = ((), (), s32[]{:S(2)}) async-start(), calls=%async_computation.1 | async-start | bytes 4325376 | tf_op jit(solution)/shard_map/all_gather | solution.py:28
  7.6 15.5 %collective-permute-start = (bf16[1,16,1,128]{3,1,2,0:T(8,128)(2,1)S(1)}, bf16[1,16,1,128]{3,1,2,0:T(8,128)(2,1)S(1)}, u32[]{:S(2)}, u32[]{:S(2)}) collective-permute-start(bf16[1,16,1,128]{3,1,2,0:T(8,128)(2,1)S(1)} %get-tuple-element.493), channel_id=1, source_target_pairs={{0,1},{1,2},{2,3},{3,4},{4,5},{5,6},{6,7},{8,9},{9,10},{10,11},{11... | collective-permute-start | bytes 12296 | tf_op jit(solution)/shard_map/ppermute | solution.py:20
  9.5 13.6 %collective-permute-start.1 = (bf16[1,16,1,128]{3,1,2,0:T(8,128)(2,1)S(1)}, bf16[1,16,1,128]{3,1,2,0:T(8,128)(2,1)S(1)}, u32[]{:S(2)}, u32[]{:S(2)}) collective-permute-start(bf16[1,16,1,128]{3,1,2,0:T(8,128)(2,1)S(1)} %get-tuple-element.494), channel_id=1, source_target_pairs={{1,0},{2,1},{3,2},{4,3},{5,4},{6,5},{7,6},{9,8},{10,9},{11,10},{12... | collective-permute-start | bytes 12296 | tf_op jit(solution)/shard_map/ppermute | solution.py:21
  27.4 6.0 collective-permute-start.2
  29.3 5.4 collective-permute-start.3
  39.6 6.3 collective-permute-start.4
  51.5 230.4 %all-gather.11.cloned.1.call-start = ((), (), s32[]{:S(2)}) async-start(), calls=%async_computation.2 | async-start | bytes 4325376 | tf_op jit(solution)/shard_map/all_gather | solution.py:28
  167.6 6.0 collective-permute-start.6
  169.5 5.0 collective-permute-start.7
  178.6 5.9 collective-permute-start.8
  190.9 6.0 collective-permute-start.10
  202.2 235.1 %all-gather.13.cloned.1.call-start = ((), (), s32[]{:S(2)}) async-start(), calls=%async_computation.3 | async-start | bytes 4325376 | tf_op jit(solution)/shard_map/all_gather | solution.py:28
  202.3 151.1 %collective-permute-start.19 = (f32[1,1,16,16,128]{4,2,3,1,0:T(8,128)S(1)}, f32[1,1,16,16,128]{4,2,3,1,0:T(8,128)S(1)}, u32[]{:S(2)}, u32[]{:S(2)}) collective-permute-start(f32[1,1,16,16,128]{4,2,3,1,0:T(8,128)S(1)} %copy.39), channel_id=1, source_target_pairs={{40,0},{48,8},{56,16},{64,24},{72,32},{80,40},{88,48},{96,56},{104... | collective-permute-start | bytes 393224 | tf_op jit(solution)/shard_map/ppermute | solution.py:41
  312.1 7.8 %collective-permute-start.12 = (f32[1,1,16,16,128]{4,2,3,1,0:T(8,128)S(1)}, f32[1,1,16,16,128]{4,2,3,1,0:T(8,128)S(1)}, u32[]{:S(2)}, u32[]{:S(2)}) collective-permute-start(f32[1,1,16,16,128]{4,2,3,1,0:T(8,128)S(1)} %bitcast_add_fusion.4), channel_id=1, source_target_pairs={{40,0},{48,8},{56,16},{64,24},{72,32},{80,40},{88,48},{96,56},{104... | collective-permute-start | bytes 393224 | tf_op jit(solution)/shard_map/ppermute | solution.py:41
  319.9 6.0 collective-permute-start.13
  321.9 5.0 collective-permute-start.14
  331.0 5.9 collective-permute-start.15
  343.2 6.0 collective-permute-start.17
  354.6 225.4 %all-reduce.15.cloned.1.call-start = ((), (), s32[]{:S(2)}) async-start(), calls=%async_computation | async-start | bytes 262144 | tf_op jit(solution)/shard_map/psum | solution.py:46
  355.3 341.9 %all-gather.15.cloned.1.call-start = ((), (), s32[]{:S(2)}) async-start(), calls=%async_computation.4 | async-start | bytes 4325376 | tf_op jit(solution)/shard_map/all_gather | solution.py:28
  580.9 6.0 collective-permute-start.20
  582.9 5.0 collective-permute-start.21
  592.0 5.9 collective-permute-start.22
  604.2 6.1 collective-permute-start.24
  (16 other events, 411.8 us)
Sparse Core Ops, SparseCore 0:
  51.6 85.6 all-gather.8
  202.4 79.5 all-gather.10
  354.7 82.6 all-gather.12
  440.6 139.2 all-reduce.14
  616.2 81.0 all-gather.14
where the time goes:
time: 745 us; the launch traced here: 735 us
  waiting for transfers between devices  455 us (61%)
  other arithmetic  131 us (18%)
  starting transfers between devices  70.8 us (10%)
  matrix products  46.1 us (6%)
  between operations  21.3 us (3%)
  local copies, waits for them, and re-layouts  7.46 us (1%)
    all_gather x4, waiting for transfers between devices, entering_2(): pieces = lax.all_gather(value, axis)  327 us
    select_n x124, other arithmetic, turn(): return jnp.where(position < mine, longer, subtotal)  118 us
    psum x1, waiting for transfers between devices, broadcast(): return lax.psum(kept, axis)  112 us
    dot_general x108, matrix products, convolve(): jnp.einsum('oc,fcrw->forw', weight[row_tap, col_tap], shifted, preferred_...  45.8 us
    ppermute x12, starting transfers between devices, extended(): before = lax.ppermute(last, axis, up)  34.2 us
    ppermute x12, starting transfers between devices, extended(): after = lax.ppermute(initial, axis, down)  33.8 us
  transfers between devices with their start and end apart: 31, of which 17 were waited for; matrix products, arithmetic and copies ran while one was open for 11% of the time, Pallas kernels for 0%

commit v1 on v0

--- a/solution.py
+++ b/solution.py
@@ -43,7 +43,7 @@
 
 def broadcast(value, axis, source):
     kept = jnp.where(lax.axis_index(axis) == source, value, 0).astype(value.dtype)
-    return lax.psum(kept, axis)
+    return jnp.sum(lax.all_gather(kept, axis), axis=0)
 
 
 def plan_table(total_steps):

time: 745 us -> 683 us (0.917)
  waiting for transfers between devices: 455 us -> 389 us
    psum x1 -> x0, waiting for transfers between devices: 112 us -> none  [broadcast(): return lax.psum(kept, axis)]
    all_gather x0 -> x1, waiting for transfers between devices: none -> 52.6 us  [broadcast(): return jnp.sum(lax.all_gather(kept, axis), axis=0)]
  transfers between devices with their start and end apart: 31 -> 31, of which waited for: 17 -> 17; matrix products, arithmetic and copies ran while one was open for 11% -> 9% of each run, Pallas kernels for 0% -> 0%
where the time goes in v1:
time: 683 us; the launch traced here: 673 us
  waiting for transfers between devices  389 us (57%)
  other arithmetic  132 us (19%)
  starting transfers between devices  70.8 us (10%)
  matrix products  48 us (7%)
  between operations  21.5 us (3%)
  local copies, waits for them, and re-layouts  8.33 us (1%)
    all_gather x4, waiting for transfers between devices, entering_2(): pieces = lax.all_gather(value, axis)  321 us
    select_n x124, other arithmetic, turn(): return jnp.where(position < mine, longer, subtotal)  118 us
    all_gather x1, waiting for transfers between devices, broadcast(): return jnp.sum(lax.all_gather(kept, axis), axis=0)  52.6 us
    dot_general x108, matrix products, convolve(): jnp.einsum('oc,fcrw->forw', weight[row_tap, col_tap], shifted, preferred_...  47.8 us
    ppermute x12, starting transfers between devices, extended(): before = lax.ppermute(last, axis, up)  34.4 us
    ppermute x12, starting transfers between devices, extended(): after = lax.ppermute(initial, axis, down)  33.6 us
  transfers between devices with their start and end apart: 31, of which 17 were waited for; matrix products, arithmetic and copies ran while one was open for 9% of the time, Pallas kernels for 0%

profile of v1, /device:TPU:8, one launch (start us, length us, event | category | flops | bytes accessed | tf_op | source)
XLA Modules:
  0.0 673.1 jit_solution(2020015299540152187)
XLA Ops:
  9.5 3.6 collective-permute-start.1
  17.2 3.2 select_reduce_fusion
  29.4 3.6 collective-permute-start.3
  39.8 3.6 collective-permute-start.4
  43.4 2.5 collective-permute-start.5
  51.7 85.8 %all-gather.11.cloned.1.call-done = f32[32,1,16,16,128]{4,3,2,1,0:T(8,128)} async-done(((f32[1,1,16,16,128]{4,3,2,1,0:T(8,128)}), f32[32,1,16,16,128]{4,3,2,1,0:T(8,128)}) %all-gather.11.cloned.1.call-update) | async-done | bytes 4194320 | tf_op jit(solution)/shard_map/all_gather | solution.py:28
  137.5 30.1 %while.56 = (s32[]{:T(128)}, f32[1,1,16,16,128]{4,3,2,1,0:T(8,128)S(1)}, s32[]{:T(128)}, f32[32,1,1,16,16,128]{5,4,3,2,1,0:T(8,128)}, s32[]{:T(128)}, /*index=5*/s32[]{:T(128)}) while((s32[]{:T(128)}, f32[1,1,16,16,128]{4,3,2,1,0:T(8,128)S(1)}, s32[]{:T(128)}, f32[32,1,1,16,16,128]{5,4,3,2,1,0:T(8,128)}, s32[]{:T(128)}, ...), condition=%wide.region_5.6_spmd.clone, body=%wide.region_4.5_spmd.clone.sunk | while | flops 98308 | bytes 393309 | solution.py:35
  169.6 3.6 collective-permute-start.7
  178.8 3.5 collective-permute-start.8
  191.0 3.5 collective-permute-start.10
  205.2 76.9 %all-gather.13.cloned.1.call-done = f32[32,1,16,16,128]{4,3,2,1,0:T(8,128)} async-done(((f32[1,1,16,16,128]{4,3,2,1,0:T(8,128)}), f32[32,1,16,16,128]{4,3,2,1,0:T(8,128)}) %all-gather.13.cloned.1.call-update) | async-done | bytes 4194320 | tf_op jit(solution)/shard_map/all_gather | solution.py:28
  282.0 30.1 %while.57 = (s32[]{:T(128)}, f32[1,1,16,16,128]{4,3,2,1,0:T(8,128)S(1)}, s32[]{:T(128)}, f32[32,1,1,16,16,128]{5,4,3,2,1,0:T(8,128)}, s32[]{:T(128)}, /*index=5*/s32[]{:T(128)}) while((s32[]{:T(128)}, f32[1,1,16,16,128]{4,3,2,1,0:T(8,128)S(1)}, s32[]{:T(128)}, f32[32,1,1,16,16,128]{5,4,3,2,1,0:T(8,128)}, s32[]{:T(128)}, ...), condition=%wide.region_7.8_spmd.clone, body=%wide.region_6.7_spmd.clone.sunk | while | flops 98308 | bytes 393309 | solution.py:35
  316.5 3.5 collective-permute-done.12
  322.0 3.6 collective-permute-start.14
  331.2 3.5 collective-permute-start.15
  343.5 3.7 collective-permute-start.17
  356.0 52.6 %all-gather.15.cloned.1.call-done = f32[32,1,16,16,128]{4,3,2,1,0:T(8,128)} async-done(((f32[1,1,16,16,128]{4,3,2,1,0:T(8,128)}), f32[32,1,16,16,128]{4,3,2,1,0:T(8,128)}) %all-gather.15.cloned.1.call-update) | async-done | bytes 4194320 | tf_op jit(solution)/shard_map/all_gather | solution.py:46
  411.0 78.6 %all-gather.17.cloned.1.call-done = f32[32,1,16,16,128]{4,3,2,1,0:T(8,128)} async-done(((f32[1,1,16,16,128]{4,3,2,1,0:T(8,128)}), f32[32,1,16,16,128]{4,3,2,1,0:T(8,128)}) %all-gather.17.cloned.1.call-update) | async-done | bytes 4194320 | tf_op jit(solution)/shard_map/all_gather | solution.py:28
  489.6 30.1 %while.58 = (s32[]{:T(128)}, f32[1,1,16,16,128]{4,3,2,1,0:T(8,128)S(1)}, s32[]{:T(128)}, f32[32,1,1,16,16,128]{5,4,3,2,1,0:T(8,128)}, s32[]{:T(128)}, /*index=5*/s32[]{:T(128)}) while((s32[]{:T(128)}, f32[1,1,16,16,128]{4,3,2,1,0:T(8,128)S(1)}, s32[]{:T(128)}, f32[32,1,1,16,16,128]{5,4,3,2,1,0:T(8,128)}, s32[]{:T(128)}, ...), condition=%wide.region_12.13_spmd.clone, body=%wide.region_11.12_spmd.clone.sunk | while | flops 98308 | bytes 393309 | solution.py:35
  521.8 3.6 collective-permute-start.21
  530.9 3.5 collective-permute-start.22
  543.1 3.5 collective-permute-start.24
  555.4 79.7 %all-gather.19.cloned.1.call-done = f32[32,1,16,16,128]{4,3,2,1,0:T(8,128)} async-done(((f32[1,1,16,16,128]{4,3,2,1,0:T(8,128)}), f32[32,1,16,16,128]{4,3,2,1,0:T(8,128)}) %all-gather.19.cloned.1.call-update) | async-done | bytes 4194320 | tf_op jit(solution)/shard_map/all_gather | solution.py:28
  635.0 30.2 %while.59 = (s32[]{:T(128)}, f32[1,1,16,16,128]{4,3,2,1,0:T(8,128)S(1)}, s32[]{:T(128)}, f32[32,1,1,16,16,128]{5,4,3,2,1,0:T(8,128)}, s32[]{:T(128)}, /*index=5*/s32[]{:T(128)}) while((s32[]{:T(128)}, f32[1,1,16,16,128]{4,3,2,1,0:T(8,128)S(1)}, s32[]{:T(128)}, f32[32,1,1,16,16,128]{5,4,3,2,1,0:T(8,128)}, s32[]{:T(128)}, ...), condition=%wide.region_14.15_spmd.clone, body=%wide.region_13.14_spmd.clone.sunk | while | flops 98308 | bytes 393309 | solution.py:35
  (357 shorter events, 223.2 us)
Async XLA Ops:
  6.5 130.9 %all-gather.11.cloned.1.call-start = ((), (), s32[]{:S(2)}) async-start(), calls=%async_computation | async-start | bytes 4325376 | tf_op jit(solution)/shard_map/all_gather | solution.py:28
  7.6 15.6 %collective-permute-start = (bf16[1,16,1,128]{3,1,2,0:T(8,128)(2,1)S(1)}, bf16[1,16,1,128]{3,1,2,0:T(8,128)(2,1)S(1)}, u32[]{:S(2)}, u32[]{:S(2)}) collective-permute-start(bf16[1,16,1,128]{3,1,2,0:T(8,128)(2,1)S(1)} %get-tuple-element.509), channel_id=1, source_target_pairs={{0,1},{1,2},{2,3},{3,4},{4,5},{5,6},{6,7},{8,9},{9,10},{10,11},{11... | collective-permute-start | bytes 12296 | tf_op jit(solution)/shard_map/ppermute | solution.py:20
  9.5 13.7 %collective-permute-start.1 = (bf16[1,16,1,128]{3,1,2,0:T(8,128)(2,1)S(1)}, bf16[1,16,1,128]{3,1,2,0:T(8,128)(2,1)S(1)}, u32[]{:S(2)}, u32[]{:S(2)}) collective-permute-start(bf16[1,16,1,128]{3,1,2,0:T(8,128)(2,1)S(1)} %get-tuple-element.510), channel_id=1, source_target_pairs={{1,0},{2,1},{3,2},{4,3},{5,4},{6,5},{7,6},{9,8},{10,9},{11,10},{12... | collective-permute-start | bytes 12296 | tf_op jit(solution)/shard_map/ppermute | solution.py:21
  27.5 6.0 collective-permute-start.2
  29.4 5.4 collective-permute-start.3
  39.8 6.4 collective-permute-start.4
  51.6 230.4 %all-gather.13.cloned.1.call-start = ((), (), s32[]{:S(2)}) async-start(), calls=%async_computation.1 | async-start | bytes 4325376 | tf_op jit(solution)/shard_map/all_gather | solution.py:28
  167.7 6.0 collective-permute-start.6
  169.6 5.0 collective-permute-start.7
  178.8 5.9 collective-permute-start.8
  191.0 6.0 collective-permute-start.10
  202.4 206.2 %all-gather.15.cloned.1.call-start = ((), (), s32[]{:S(2)}) async-start(), calls=%async_computation.2 | async-start | bytes 4325376 | tf_op jit(solution)/shard_map/all_gather | solution.py:46
  203.1 150.8 %collective-permute-start.19 = (f32[1,1,16,16,128]{4,2,3,1,0:T(8,128)}, f32[1,1,16,16,128]{4,2,3,1,0:T(8,128)}, u32[]{:S(2)}, u32[]{:S(2)}) collective-permute-start(f32[1,1,16,16,128]{4,2,3,1,0:T(8,128)} %copy.58), channel_id=1, source_target_pairs={{40,0},{48,8},{56,16},{64,24},{72,32},{80,40},{88,48},{96,56},{104... | collective-permute-start | bytes 393224 | tf_op jit(solution)/shard_map/ppermute | solution.py:41
  312.3 7.8 %collective-permute-start.12 = (f32[1,1,16,16,128]{4,2,3,1,0:T(8,128)S(1)}, f32[1,1,16,16,128]{4,2,3,1,0:T(8,128)S(1)}, u32[]{:S(2)}, u32[]{:S(2)}) collective-permute-start(f32[1,1,16,16,128]{4,2,3,1,0:T(8,128)S(1)} %bitcast_add_fusion.6), channel_id=1, source_target_pairs={{40,0},{48,8},{56,16},{64,24},{72,32},{80,40},{88,48},{96,56},{104... | collective-permute-start | bytes 393224 | tf_op jit(solution)/shard_map/ppermute | solution.py:41
  320.1 6.8 %collective-permute-start.13 = (bf16[1,16,1,128]{3,1,2,0:T(8,128)(2,1)S(1)}, bf16[1,16,1,128]{3,1,2,0:T(8,128)(2,1)S(1)}, u32[]{:S(2)}, u32[]{:S(2)}) collective-permute-start(bf16[1,16,1,128]{3,1,2,0:T(8,128)(2,1)S(1)} %get-tuple-element.505), channel_id=1, source_target_pairs={{0,1},{1,2},{2,3},{3,4},{4,5},{5,6},{6,7},{8,9},{9,10},{10,11},{11... | collective-permute-start | bytes 12296 | tf_op jit(solution)/shard_map/ppermute | solution.py:20
  322.0 5.0 collective-permute-start.14
  326.8 162.8 %all-gather.17.cloned.1.call-start = ((), (), s32[]{:S(2)}) async-start(), calls=%async_computation.3 | async-start | bytes 4325376 | tf_op jit(solution)/shard_map/all_gather | solution.py:28
  331.2 5.9 collective-permute-start.15
  343.5 6.0 collective-permute-start.17
  355.9 279.1 %all-gather.19.cloned.1.call-start = ((), (), s32[]{:S(2)}) async-start(), calls=%async_computation.4 | async-start | bytes 4325376 | tf_op jit(solution)/shard_map/all_gather | solution.py:28
  519.8 6.0 collective-permute-start.20
  521.8 5.0 collective-permute-start.21
  530.9 5.9 collective-permute-start.22
  543.1 6.1 collective-permute-start.24
  (16 other events, 523.1 us)
Sparse Core Ops, SparseCore 0:
  51.8 85.6 all-gather.10
  202.5 79.5 all-gather.12
  326.9 81.6 all-gather.14
  411.0 78.5 all-gather.16
  555.5 79.5 all-gather.18
